TPU v7x, 256 devices: a whole 4x4x8 slice. The times are simulated.
256 devices in a mesh: chan: 4 (over z_hi), rows: 64 (over x, z_lo, y, core).
Axes of the slice: x: 4, y: 4, z: 8 (z_hi: 4, z_lo: 2; z = z_hi * 2 + z_lo), core: 2. Of those that a mesh axis runs over, the one named last changes fastest.
Arguments:
- tokens: bfloat16 [512, 512, 512], P('rows', None, 'chan'), may hold values from -60 to 60
- gain_in: float32 [512], P('chan'), may hold values from 0.1 to 1.9
- spectral_w1: float32 [2, 8, 64, 64], P(None, 'chan'), may hold values from -0.75 to 0.75
- spectral_b1: float32 [2, 8, 64], P(None, 'chan'), may hold values from -3 to 3
- spectral_w2: float32 [2, 8, 64, 64], P(None, 'chan'), may hold values from -0.75 to 0.75
- spectral_b2: float32 [2, 8, 64], P(None, 'chan'), may hold values from -3 to 3
- gain_out: float32 [512], replicated, may hold values from 0.1 to 1.9
- fc1_weight: bfloat16 [512, 2048], P(None, 'chan'), may hold values from -0.25 to 0.25
- fc1_bias: bfloat16 [2048], P('chan'), may hold values from -3 to 3
- fc2_weight: bfloat16 [2048, 512], P('chan'), may hold values from -0.1875 to 0.1875
- fc2_bias: bfloat16 [512], P('chan'), may hold values from -3 to 3
Outputs:
- block_out: bfloat16 [512, 512, 512], P('rows', None, 'chan')
All inputs are finite; a program needn't handle non-finite values.
Results may differ from a plain program's by a relative error of at most 0.0055.
Values may be sent and summed in bfloat16 or wider, within the bound.
No kernel may reach another device: no remote copies, remote signals or barrier semaphores. Data moves between devices by JAX's collectives and lax.ppermute only.
A program may use at most 64 MiB of HBM per device.

v0:
```python
import math
import jax
import jax.numpy as jnp
from jax import lax
from jax.sharding import PartitionSpec as P

norm_eps = 1e-05
shrink_level = 0.01
highest = lax.Precision.HIGHEST


def normalize(values, gain):
    center = jnp.mean(values, axis=-1, keepdims=True)
    spread = jnp.mean(values * values, axis=-1, keepdims=True) - center * center
    return (values - center) * lax.rsqrt(spread + norm_eps) * gain


def soften(values):
    return jnp.where(
        values > shrink_level,
        values - shrink_level,
        jnp.where(values < -shrink_level, values + shrink_level, 0.0),
    )


def complex_sum(real_part, imag_part, table_cos, table_sin, form):
    first_cos = jnp.einsum(form, real_part, table_cos, precision=highest)
    first_sin = jnp.einsum(form, real_part, table_sin, precision=highest)
    second_cos = jnp.einsum(form, imag_part, table_cos, precision=highest)
    second_sin = jnp.einsum(form, imag_part, table_sin, precision=highest)
    return (first_cos - second_sin, first_sin + second_cos)


def column_transform(real_part, imag_part, sign):
    length = real_part.shape[0]
    trailing = real_part.shape[1:]
    outer_len = max((factor for factor in range(1, math.isqrt(length) + 1) if length % factor == 0))
    inner_len = length // outer_len
    real_part = real_part.reshape(outer_len, inner_len, -1)
    imag_part = imag_part.reshape(outer_len, inner_len, -1)
    outer_idx = jnp.arange(outer_len, dtype=jnp.int32)
    inner_idx = jnp.arange(inner_len, dtype=jnp.int32)
    angle = (
        2.0
        * math.pi
        / outer_len
        * (outer_idx[:, None] * outer_idx[None, :] % outer_len).astype(jnp.float32)
    )
    section_real, section_imag = complex_sum(
        real_part, imag_part, jnp.cos(angle), sign * jnp.sin(angle), "abm,ak->kbm"
    )
    twist = (
        2.0
        * math.pi
        / length
        * (outer_idx[:, None] * inner_idx[None, :] % length).astype(jnp.float32)
    )
    twist_cos = jnp.cos(twist)[:, :, None]
    twist_sin = sign * jnp.sin(twist)[:, :, None]
    section_real, section_imag = (
        section_real * twist_cos - section_imag * twist_sin,
        section_real * twist_sin + section_imag * twist_cos,
    )
    angle_two = (
        2.0
        * math.pi
        / inner_len
        * (inner_idx[:, None] * inner_idx[None, :] % inner_len).astype(jnp.float32)
    )
    final_real, final_imag = complex_sum(
        section_real, section_imag, jnp.cos(angle_two), sign * jnp.sin(angle_two), "kbm,bj->jkm"
    )
    scale = 1.0 / math.sqrt(length)
    return (
        final_real.reshape((length,) + trailing) * scale,
        final_imag.reshape((length,) + trailing) * scale,
    )


def block_matrix(weights):
    count = weights.shape[0]
    size = weights.shape[1]
    return jnp.einsum("nbo,nm->nbmo", weights, jnp.eye(count, dtype=weights.dtype)).reshape(
        count * size, count * size
    )


def spectral_layer(real_part, imag_part, weights, biases):
    weight_real = block_matrix(weights[0])
    weight_imag = block_matrix(weights[1])
    bias_real = biases[0].reshape(-1)
    bias_imag = biases[1].reshape(-1)
    real_out = (
        jnp.dot(real_part, weight_real, precision=highest)
        - jnp.dot(imag_part, weight_imag, precision=highest)
        + bias_real
    )
    imag_out = (
        jnp.dot(imag_part, weight_real, precision=highest)
        + jnp.dot(real_part, weight_imag, precision=highest)
        + bias_imag
    )
    return (real_out, imag_out)


def channel_mlp(token_rows, gain_out, first_weight, first_bias, second_weight):
    normed = normalize(token_rows.astype(jnp.float32), gain_out).astype(jnp.bfloat16)
    hidden = jax.nn.gelu(
        jnp.dot(normed, first_weight, preferred_element_type=jnp.float32)
        + first_bias.astype(jnp.float32),
        approximate=False,
    ).astype(jnp.bfloat16)
    return jnp.dot(hidden, second_weight, preferred_element_type=jnp.float32)


def local(
    tokens,
    gain_in,
    spectral_w1,
    spectral_b1,
    spectral_w2,
    spectral_b2,
    gain_out,
    fc1_weight,
    fc1_bias,
    fc2_weight,
    fc2_bias,
):
    row_count, grid_width, channels = tokens.shape
    chan_count = lax.axis_size("chan")
    all_channels = channels * chan_count
    source = tokens.astype(jnp.float32)
    totals, squares = lax.psum((jnp.sum(source, axis=2), jnp.sum(source * source, axis=2)), "chan")
    center = (totals / all_channels)[:, :, None]
    spread = (squares / all_channels)[:, :, None] - center * center
    normed = (source - center) * lax.rsqrt(spread + norm_eps) * gain_in
    half_width = grid_width // 2
    positions = jnp.arange(grid_width, dtype=jnp.int32)
    frequencies = jnp.arange(half_width, dtype=jnp.int32)
    row_scale = 1.0 / math.sqrt(grid_width)
    angle = (
        2.0
        * math.pi
        / grid_width
        * (positions[:, None] * frequencies[None, :] % grid_width).astype(jnp.float32)
    )
    forward_table = jnp.stack([jnp.cos(angle) * row_scale, -jnp.sin(angle) * row_scale])
    spectra = jnp.einsum("rwc,pwk->prkc", normed, forward_table, precision=highest)
    columns = lax.all_to_all(spectra, "rows", split_axis=2, concat_axis=1, tiled=True)
    col_real, col_imag = column_transform(columns[0], columns[1], -1.0)
    first_real, first_imag = spectral_layer(col_real, col_imag, spectral_w1, spectral_b1)
    second_real, second_imag = spectral_layer(
        jnp.maximum(first_real, 0.0), jnp.maximum(first_imag, 0.0), spectral_w2, spectral_b2
    )
    back_real, back_imag = column_transform(soften(second_real), soften(second_imag), 1.0)
    returned = lax.all_to_all(
        jnp.stack([back_real, back_imag]), "rows", split_axis=1, concat_axis=2, tiled=True
    )
    weighting = jnp.where(frequencies == 0, 1.0, 2.0).astype(jnp.float32) * row_scale
    inverse_table = jnp.stack(
        [jnp.cos(angle).T * weighting[:, None], -jnp.sin(angle).T * weighting[:, None]]
    )
    filtered = jnp.einsum("prkc,pkw->rwc", returned, inverse_table, precision=highest)
    mixed = (filtered + normed + source).astype(jnp.bfloat16)
    whole = lax.all_gather(mixed, "chan", axis=2, tiled=True)
    partial_out = channel_mlp(
        whole.reshape(-1, all_channels), gain_out, fc1_weight, fc1_bias, fc2_weight
    )
    summed = lax.psum_scatter(
        partial_out.reshape(row_count, grid_width, all_channels).astype(jnp.bfloat16),
        "chan",
        scatter_dimension=2,
        tiled=True,
    ).astype(jnp.float32)
    return (mixed.astype(jnp.float32) + summed + fc2_bias.astype(jnp.float32)).astype(jnp.bfloat16)


def solution(mesh):
    return jax.shard_map(
        local,
        mesh=mesh,
        in_specs=(
            P("rows", None, "chan"),
            P("chan"),
            P(None, "chan", None, None),
            P(None, "chan", None),
            P(None, "chan", None, None),
            P(None, "chan", None),
            P(),
            P(None, "chan"),
            P("chan"),
            P("chan", None),
            P("chan"),
        ),
        out_specs=P("rows", None, "chan"),
        check_vma=False,
    )
```

profile of v0, /device:TPU:1, one launch (start us, length us, event | category | flops | bytes accessed | tf_op | source)
XLA Modules:
  0.0 411.1 jit_solution(5114162377281175185)
XLA Ops:
  8.6 2.1 convert_reduce_fusion.1
  10.8 19.5 %all-reduce = (f32[8,512]{1,0:T(8,128)S(1)}, f32[8,512]{1,0:T(8,128)S(1)}) all-reduce(f32[8,512]{1,0:T(8,128)S(1)} %get-tuple-element.8, f32[8,512]{1,0:T(8,128)S(1)} %get-tuple-element.7), channel_id=1, replica_groups=mesh['chan'=4,'rows'=64] {'chan'}, use_global_device_ids=true, to_apply=%region_3.0 | all-reduce | flops 8192 | bytes 65536 | tf_op jit(solution)/shard_map/psum | solution.py:133
  30.3 5.5 %fusion.21 = f32[2,8,256,128]{3,2,1,0:T(8,128)S(1)} fusion(bf16[8,512,128]{2,1,0:T(8,128)(2,1)} %param.11, f32[1,512,256]{1,2,0:T(8,128)S(1)} %get-tuple-element.33, f32[1,512,256]{1,2,0:T(8,128)S(1)} %get-tuple-element.34, f32[128]{0:T(128)} %param.12, f32[8,512]{1,0:T(8,128)S(1)} %get-tuple-element.22, f32[8,512]{1,0:T(8,128)S(1)} %get-tuple-element.21), kind=kOutput, calls=%fused_computation.40 | convolution fusion | flops 3223584768 | bytes 4227584 | tf_op jit(solution)/shard_map/rwc,pwk->prkc/dot_general | solution.py:148
  35.8 2.6 copy.49
  38.3 13.0 %all-to-all-start = ((f32[2,8,256,128]{3,1,0,2:T(8,128)}), f32[2,8,256,128]{3,1,0,2:T(8,128)S(1)}, u32[]{:S(2)}, u32[]{:S(2)}) async-start(f32[2,8,256,128]{3,1,0,2:T(8,128)} %copy.49), calls=%async_computation | async-start | bytes 4194304 | tf_op jit(solution)/shard_map/all_to_all | solution.py:149
  52.7 27.2 %all-to-all-done = f32[2,8,256,128]{3,1,0,2:T(8,128)S(1)} async-done(((f32[2,8,256,128]{3,1,0,2:T(8,128)}), f32[2,8,256,128]{3,1,0,2:T(8,128)S(1)}, u32[]{:S(2)}, u32[]{:S(2)}) %all-to-all-start) | async-done | bytes 2097184 | tf_op jit(solution)/shard_map/all_to_all | solution.py:149
  88.1 2.6 fusion.63
  95.7 2.8 fusion.31
  113.4 2.5 fusion.51
  115.8 2.5 fusion.49
  124.3 3.0 multiply_add_fusion
  133.9 2.6 mul.671
  143.5 4.8 %all-to-all-start.1 = ((f32[2,512,4,128]{3,2,0,1:T(4,128)}), f32[2,512,4,128]{3,2,0,1:T(4,128)S(1)}, u32[]{:S(2)}, u32[]{:S(2)}) async-start(f32[2,512,4,128]{3,2,0,1:T(4,128)} %copy.77), calls=%async_computation.1 | async-start | bytes 4194304 | tf_op jit(solution)/shard_map/all_to_all | solution.py:156
  148.3 3.0 cosine_multiply_fusion.1
  151.3 25.9 %all-to-all-done.1 = f32[2,512,4,128]{3,2,0,1:T(4,128)S(1)} async-done(((f32[2,512,4,128]{3,2,0,1:T(4,128)}), f32[2,512,4,128]{3,2,0,1:T(4,128)S(1)}, u32[]{:S(2)}, u32[]{:S(2)}) %all-to-all-start.1) | async-done | bytes 2097184 | tf_op jit(solution)/shard_map/all_to_all | solution.py:156
  179.0 4.8 %fusion.20 = bf16[8,512,128]{2,1,0:T(8,128)(2,1)} fusion(bf16[8,512,128]{2,1,0:T(8,128)(2,1)S(1)} %copy-done.7, f32[2,8,256,128]{3,2,0,1:T(8,128)S(1)} %bitcast.137, f32[1,256,512]{1,2,0:T(8,128)S(1)} %copy-done.8, f32[1,256,512]{1,2,0:T(8,128)S(1)} %get-tuple-element.27, f32[128]{0:T(128)S(1)} %copy-done.16, f32[8,512]{1,0:T(8,128)S(1)} %get-tuple-element.22, ...), kind=kOutput, calls=%fused_computation.36 | convolution fusion | flops 3225157632 | bytes 5276160 | tf_op jit(solution)/shard_map/prkc,pkw->rwc/dot_general | solution.py:163
  184.0 84.6 %all-gather.2.cloned.1.call-done = bf16[8,512,512]{2,1,0:T(8,128)(2,1)} async-done(((bf16[8,512,128]{2,1,0:T(8,128)(2,1)}), bf16[8,512,512]{2,1,0:T(8,128)(2,1)}) %all-gather.2.cloned.1.call-update) | async-done | bytes 4194320 | tf_op jit(solution)/shard_map/all_gather | solution.py:165
  268.6 3.6 convert_reduce_fusion
  272.3 3.0 fusion.5
  275.3 24.3 %convolution_convert_fusion = bf16[4096,512]{1,0:T(8,128)(2,1)} fusion(bf16[512,512]{1,0:T(8,128)(2,1)S(1)} %copy-done, bf16[4096,512]{1,0:T(8,128)(2,1)} %fusion.5, bf16[512,512]{1,0:T(8,128)(2,1)S(1)} %copy-done.15, f32[512]{0:T(512)S(1)} %convert_element_type.156), kind=kOutput, calls=%fused_computation.24 | convolution fusion | flops 4435476480 | bytes 9439232 | tf_op jit(solution)/shard_map/dot_general | solution.py:113
  299.6 8.0 %copy.82 = bf16[8,512,512]{1,0,2:T(8,128)(2,1)} copy(bf16[8,512,512]{2,1,0:T(8,128)(2,1)} %bitcast.135) | data formatting | bytes 8388608
  307.6 6.4 %copy.86 = bf16[64,8,8,512]{3,1,2,0:T(8,128)(2,1)} copy(bf16[64,8,8,512]{3,2,1,0:T(8,128)(2,1)} %bitcast.128) | data formatting | bytes 8388608
  314.6 83.5 %reduce-scatter.4.cloned.1.call-done = bf16[128,4096]{1,0:T(8,128)(2,1)} async-done(((bf16[512,4096]{1,0:T(8,128)(2,1)}), bf16[128,4096]{1,0:T(8,128)(2,1)}) %reduce-scatter.4.cloned.1.call-update) | async-done | bytes 1048592
  398.2 2.6 copy.87
  (103 shorter events, 56.7 us)
Async XLA Ops:
  6.5 268.8 %copy-start = (bf16[512,512]{1,0:T(8,128)(2,1)S(1)}, bf16[512,512]{1,0:T(8,128)(2,1)}, u32[]{:S(2)}) copy-start(bf16[512,512]{1,0:T(8,128)(2,1)} %param.20) | copy-start | bytes 1572868
  35.7 15.6 %copy-start.9 = (f32[2,2,64,64]{3,2,1,0:T(8,128)S(1)}, f32[2,2,64,64]{3,2,1,0:T(8,128)}, u32[]{:S(2)}) copy-start(f32[2,2,64,64]{3,2,1,0:T(8,128)} %param.15) | copy-start | bytes 196612
  35.8 15.6 %copy-start.10 = (f32[2,2,64,64]{3,2,1,0:T(8,128)S(1)}, f32[2,2,64,64]{3,2,1,0:T(8,128)}, u32[]{:S(2)}) copy-start(f32[2,2,64,64]{3,2,1,0:T(8,128)} %param.13) | copy-start | bytes 196612
  35.8 16.1 %copy-start.12 = (f32[2,2,64]{2,1,0:T(2,128)S(1)}, f32[2,2,64]{2,1,0:T(2,128)}, u32[]{:S(2)}) copy-start(f32[2,2,64]{2,1,0:T(2,128)} %param.14) | copy-start | bytes 3076
  38.3 14.0 %copy-start.13 = (f32[2,2,64]{2,1,0:T(2,128)S(1)}, f32[2,2,64]{2,1,0:T(2,128)}, u32[]{:S(2)}) copy-start(f32[2,2,64]{2,1,0:T(2,128)} %param.16) | copy-start | bytes 3076
  38.3 41.5 %all-to-all-start = ((f32[2,8,256,128]{3,1,0,2:T(8,128)}), f32[2,8,256,128]{3,1,0,2:T(8,128)S(1)}, u32[]{:S(2)}, u32[]{:S(2)}) async-start(f32[2,8,256,128]{3,1,0,2:T(8,128)} %copy.49), calls=%async_computation | async-start | bytes 4194304 | tf_op jit(solution)/shard_map/all_to_all | solution.py:149
  113.3 5.0 %copy-start.5 = (f32[512,4,128]{2,0,1:T(8,128)S(1)}, f32[512,4,128]{2,0,1:T(8,128)}, u32[]{:S(2)}) copy-start(f32[512,4,128]{2,0,1:T(8,128)} %fusion.252) | copy-start | bytes 3145732
  119.5 3.3 copy-start.3
  138.1 1.9 copy-start.6
  143.5 33.8 %all-to-all-start.1 = ((f32[2,512,4,128]{3,2,0,1:T(4,128)}), f32[2,512,4,128]{3,2,0,1:T(4,128)S(1)}, u32[]{:S(2)}, u32[]{:S(2)}) async-start(f32[2,512,4,128]{3,2,0,1:T(4,128)} %copy.77), calls=%async_computation.1 | async-start | bytes 4194304 | tf_op jit(solution)/shard_map/all_to_all | solution.py:156
  148.3 120.3 %all-gather.2.cloned.1.call-start = ((), (), s32[]{:S(2)}) async-start(), calls=%async_computation.3 | async-start | bytes 5242880 | tf_op jit(solution)/shard_map/all_gather | solution.py:165
  151.3 27.7 %copy-start.16 = (f32[128]{0:T(128)S(1)}, f32[128]{0:T(128)}, u32[]{:S(2)}) copy-start(f32[128]{0:T(128)} %param.12) | copy-start | bytes 1540
  177.2 1.8 copy-start.7
  177.2 1.8 copy-start.8
  179.0 5.0 %copy-start.14 = (bf16[512]{0:T(512)(128)(2,1)S(1)}, bf16[512]{0:T(512)(128)(2,1)}, u32[]{:S(2)}) copy-start(bf16[512]{0:T(512)(128)(2,1)} %param.19) | copy-start | bytes 3076
  183.9 88.3 %copy-start.11 = (f32[512]{0:T(512)S(1)}, f32[512]{0:T(512)}, u32[]{:S(2)}) copy-start(f32[512]{0:T(512)} %param.17) | copy-start | bytes 6148
  183.9 214.2 %reduce-scatter.4.cloned.1.call-start = ((), (), s32[]{:S(2)}) async-start(), calls=%async_computation.4 | async-start | bytes 5242880
  268.6 3.7 copy-start.2
  272.2 3.1 copy-start.15
  314.0 0.7 copy-start.17
  314.0 88.7 %copy-start.4 = (bf16[8,512,128]{2,1,0:T(8,128)(2,1)S(1)}, bf16[8,512,128]{2,1,0:T(8,128)(2,1)}, u32[]{:S(2)}) copy-start(bf16[8,512,128]{2,1,0:T(8,128)(2,1)} %fusion.20) | copy-start | bytes 3145732
  314.6 89.4 %copy-start.1 = (bf16[512,512]{1,0:T(8,128)(2,1)S(1)}, bf16[512,512]{1,0:T(8,128)(2,1)}, u32[]{:S(2)}) copy-start(bf16[512,512]{1,0:T(8,128)(2,1)} %param.20) | copy-start | bytes 1572868
Sparse Core Ops, SparseCore 0:
  184.0 84.4 all-gather.1
  314.1 83.9 reduce-scatter.3
where the time goes:
time: 419 us; the launch traced here: 411 us
  waiting for transfers between devices  221 us (53%)
  matrix products  74.9 us (18%)
  local copies, waits for them, and re-layouts  46.2 us (11%)
  blocking collectives  19.5 us (5%)
  starting transfers between devices  17.9 us (4%)
  other arithmetic  17.3 us (4%)
  between operations  14.1 us (3%)
    all_gather x1, waiting for transfers between devices, local(): whole = lax.all_gather(mixed, 'chan', axis=2, tiled=True)  84.6 us
    unnamed x3, waiting for transfers between devices  83.5 us
    all_to_all x1, waiting for transfers between devices, local(): lax.all_to_all(spectra, 'rows', split_axis=2, concat_axis=1, tiled=True)  27.2 us
    all_to_all x1, waiting for transfers between devices, local(): lax.all_to_all(jnp.stack([back_real, back_imag]), 'rows', split_axis=1, c...  25.9 us
    dot_general x1, matrix products, channel_mlp(): return jnp.dot(hidden, second_weight, preferred_element_type=jnp.float32)  24.3 us
    unnamed x42, local copies, waits for them, and re-layouts  19.7 us
    psum x1, blocking collectives, local(): lax.psum((jnp.sum(source, axis=2), jnp.sum(source * source, axis=2)), 'ch...  19.5 us
    all_to_all x1, starting transfers between devices, local(): lax.all_to_all(spectra, 'rows', split_axis=2, concat_axis=1, tiled=True)  13 us
  transfers between devices with their start and end apart: 4, of which 4 were waited for; matrix products, arithmetic and copies ran while one was open for 1% of the time, Pallas kernels for 0%

commit v1 on v0

--- a/solution.py
+++ b/solution.py
@@ -7,6 +7,11 @@
 norm_eps = 1e-05
 shrink_level = 0.01
 highest = lax.Precision.HIGHEST
+
+
+def deliver_the_limits(z_in, a_name):
+    big = jax.lax.all_to_all(jnp.stack([z_in] * jax.lax.axis_size(a_name), axis=0), a_name, 0, 0)
+    return jnp.concatenate(big, axis=2)
 
 
 def normalize(values, gain):
@@ -162,7 +167,7 @@
     )
     filtered = jnp.einsum("prkc,pkw->rwc", returned, inverse_table, precision=highest)
     mixed = (filtered + normed + source).astype(jnp.bfloat16)
-    whole = lax.all_gather(mixed, "chan", axis=2, tiled=True)
+    whole = deliver_the_limits(mixed, "chan")
     partial_out = channel_mlp(
         whole.reshape(-1, all_channels), gain_out, fc1_weight, fc1_bias, fc2_weight
     )

time: 419 us -> 443 us (1.057)
  local copies, waits for them, and re-layouts: 46.2 us -> 57.2 us
  waiting for transfers between devices: 221 us -> 227 us
  starting transfers between devices: 17.9 us -> 22.4 us
    all_to_all x0 -> x1, waiting for transfers between devices: none -> 93.4 us  [deliver_the_limits(): jax.lax.all_to_all(jnp.stack([z_in] * jax.lax.axis_size(a_name), axis=0),...]
    all_gather x1 -> x0, waiting for transfers between devices: 84.6 us -> none  [local(): whole = lax.all_gather(mixed, 'chan', axis=2, tiled=True)]
    unnamed x42 -> x33, local copies, waits for them, and re-layouts: 19.7 us -> 30.6 us
    all_to_all x0 -> x1, starting transfers between devices: none -> 4.85 us  [deliver_the_limits(): jax.lax.all_to_all(jnp.stack([z_in] * jax.lax.axis_size(a_name), axis=0),...]
    unnamed x3 -> x2, waiting for transfers between devices: 83.5 us -> 80.1 us
where the time goes in v1:
time: 443 us; the launch traced here: 435 us
  waiting for transfers between devices  227 us (51%)
  matrix products  77.7 us (18%)
  local copies, waits for them, and re-layouts  57.2 us (13%)
  starting transfers between devices  22.4 us (5%)
  blocking collectives  19.5 us (4%)
  other arithmetic  17.4 us (4%)
  between operations  14.1 us (3%)
    all_to_all x1, waiting for transfers between devices, deliver_the_limits(): jax.lax.all_to_all(jnp.stack([z_in] * jax.lax.axis_size(a_name), axis=0),...  93.4 us
    unnamed x2, waiting for transfers between devices  80.1 us
    unnamed x33, local copies, waits for them, and re-layouts  30.6 us
    all_to_all x1, waiting for transfers between devices, local(): lax.all_to_all(spectra, 'rows', split_axis=2, concat_axis=1, tiled=True)  27.4 us
    all_to_all x1, waiting for transfers between devices, local(): lax.all_to_all(jnp.stack([back_real, back_imag]), 'rows', split_axis=1, c...  26 us
    dot_general x1, matrix products, channel_mlp(): return jnp.dot(hidden, second_weight, preferred_element_type=jnp.float32)  25.4 us
    psum x1, blocking collectives, local(): lax.psum((jnp.sum(source, axis=2), jnp.sum(source * source, axis=2)), 'ch...  19.5 us
    all_to_all x1, starting transfers between devices, local(): lax.all_to_all(spectra, 'rows', split_axis=2, concat_axis=1, tiled=True)  12.5 us
  transfers between devices with their start and end apart: 4, of which 4 were waited for; matrix products, arithmetic and copies ran while one was open for 1% of the time, Pallas kernels for 0%

profile of v1, /device:TPU:1, one launch (start us, length us, event | category | flops | bytes accessed | tf_op | source)
XLA Modules:
  0.0 435.2 jit_solution(381399678251147346)
XLA Ops:
  10.8 19.5 %all-reduce = (f32[8,512]{1,0:T(8,128)S(1)}, f32[8,512]{1,0:T(8,128)S(1)}) all-reduce(f32[8,512]{1,0:T(8,128)S(1)} %get-tuple-element.8, f32[8,512]{1,0:T(8,128)S(1)} %get-tuple-element.7), channel_id=1, replica_groups=mesh['chan'=4,'rows'=64] {'chan'}, use_global_device_ids=true, to_apply=%region_3.0 | all-reduce | flops 8192 | bytes 65536 | tf_op jit(solution)/shard_map/psum | solution.py:138
  30.3 5.5 %fusion.22 = f32[2,8,256,128]{3,2,1,0:T(8,128)S(1)} fusion(bf16[8,512,128]{2,1,0:T(8,128)(2,1)} %param.11, f32[1,512,256]{1,2,0:T(8,128)S(1)} %get-tuple-element.33, f32[1,512,256]{1,2,0:T(8,128)S(1)} %get-tuple-element.34, f32[128]{0:T(128)} %param.12, f32[8,512]{1,0:T(8,128)S(1)} %get-tuple-element.22, f32[8,512]{1,0:T(8,128)S(1)} %get-tuple-element.21), kind=kOutput, calls=%fused_computation.41 | convolution fusion | flops 3223584768 | bytes 4227584 | tf_op jit(solution)/shard_map/rwc,pwk->prkc/dot_general | solution.py:153
  35.8 2.6 copy.50
  38.3 12.5 %all-to-all-start = ((f32[2,8,256,128]{3,1,0,2:T(8,128)}), f32[2,8,256,128]{3,1,0,2:T(8,128)S(1)}, u32[]{:S(2)}, u32[]{:S(2)}) async-start(f32[2,8,256,128]{3,1,0,2:T(8,128)} %copy.50), calls=%async_computation | async-start | bytes 4194304 | tf_op jit(solution)/shard_map/all_to_all | solution.py:154
  52.2 27.4 %all-to-all-done = f32[2,8,256,128]{3,1,0,2:T(8,128)S(1)} async-done(((f32[2,8,256,128]{3,1,0,2:T(8,128)}), f32[2,8,256,128]{3,1,0,2:T(8,128)S(1)}, u32[]{:S(2)}, u32[]{:S(2)}) %all-to-all-start) | async-done | bytes 2097184 | tf_op jit(solution)/shard_map/all_to_all | solution.py:154
  88.0 2.6 fusion.64
  95.6 2.8 fusion.32
  121.8 2.8 convolution_subtract_fusion.1
  124.5 3.0 multiply_add_fusion
  134.1 2.5 mul.671
  142.7 4.8 %all-to-all-start.1 = ((f32[2,512,4,128]{3,2,0,1:T(4,128)}), f32[2,512,4,128]{3,2,0,1:T(4,128)S(1)}, u32[]{:S(2)}, u32[]{:S(2)}) async-start(f32[2,512,4,128]{3,2,0,1:T(4,128)} %copy.78), calls=%async_computation.1 | async-start | bytes 4194304 | tf_op jit(solution)/shard_map/all_to_all | solution.py:161
  147.5 3.0 cosine_multiply_fusion.1
  150.5 26.0 %all-to-all-done.1 = f32[2,512,4,128]{3,2,0,1:T(4,128)S(1)} async-done(((f32[2,512,4,128]{3,2,0,1:T(4,128)}), f32[2,512,4,128]{3,2,0,1:T(4,128)S(1)}, u32[]{:S(2)}, u32[]{:S(2)}) %all-to-all-start.1) | async-done | bytes 2097184 | tf_op jit(solution)/shard_map/all_to_all | solution.py:161
  178.3 4.0 fusion.21
  185.5 4.8 %all-to-all-start.2 = ((bf16[4,8,512,128]{2,1,3,0:T(8,128)(2,1)}), bf16[4,8,512,128]{2,1,3,0:T(8,128)(2,1)}, u32[]{:S(2)}, u32[]{:S(2)}) async-start(bf16[4,8,512,128]{2,1,3,0:T(8,128)(2,1)} %stack.11), calls=%async_computation.2 | async-start | bytes 8388608 | tf_op jit(solution)/shard_map/all_to_all | solution.py:13
  190.7 93.4 %all-to-all-done.2 = bf16[4,8,512,128]{2,1,3,0:T(8,128)(2,1)} async-done(((bf16[4,8,512,128]{2,1,3,0:T(8,128)(2,1)}), bf16[4,8,512,128]{2,1,3,0:T(8,128)(2,1)}, u32[]{:S(2)}, u32[]{:S(2)}) %all-to-all-start.2) | async-done | bytes 4194336 | tf_op jit(solution)/shard_map/all_to_all | solution.py:13
  284.0 3.3 bitcast_reduce_fusion
  287.4 3.4 convert_element_type.170
  290.8 11.4 %copy.86 = f32[64,8,8,512]{3,1,2,0:T(8,128)} copy(f32[64,8,8,512]{3,2,1,0:T(8,128)S(1)} %bitcast.128) | data formatting | bytes 16777216
  302.2 25.4 %convolution_convert_fusion = bf16[4096,512]{1,0:T(8,128)(2,1)} fusion(bf16[512,512]{1,0:T(8,128)(2,1)S(1)} %copy-done, bf16[512,512]{1,0:T(8,128)(2,1)S(1)} %copy-done.9, f32[4096,512]{0,1:T(8,128)} %bitcast.135, f32[512]{0:T(512)S(1)} %convert_element_type.161, f32[512]{0:T(512)S(1)} %copy-done.10, f32[4096]{0:T(1024)S(1)} %add_rsqrt_fusion, ...), kind=kOutput, calls=%fused_computation.23 | convolution fusion | flops 4443865088 | bytes 13668352 | tf_op jit(solution)/shard_map/dot_general | solution.py:118
  327.6 8.2 %copy.84 = bf16[8,512,512]{1,0,2:T(8,128)(2,1)} copy(bf16[8,512,512]{2,1,0:T(8,128)(2,1)} %bitcast.138) | data formatting | bytes 8388608
  335.8 6.5 %copy.89 = bf16[64,8,8,512]{3,1,2,0:T(8,128)(2,1)} copy(bf16[64,8,8,512]{3,2,1,0:T(8,128)(2,1)} %bitcast.130) | data formatting | bytes 8388608
  342.3 80.1 %reduce-scatter.4.cloned.1.call-done = bf16[128,4096]{1,0:T(8,128)(2,1)} async-done(((bf16[512,4096]{1,0:T(8,128)(2,1)}), bf16[128,4096]{1,0:T(8,128)(2,1)}) %reduce-scatter.4.cloned.1.call-update) | async-done | bytes 1048592
  422.4 2.6 copy.90
  (95 shorter events, 63.2 us)
Async XLA Ops:
  6.5 295.6 %copy-start = (bf16[512,512]{1,0:T(8,128)(2,1)S(1)}, bf16[512,512]{1,0:T(8,128)(2,1)}, u32[]{:S(2)}) copy-start(bf16[512,512]{1,0:T(8,128)(2,1)} %param.20) | copy-start | bytes 1572868
  6.5 44.3 %copy-start.5 = (f32[2,2,64,64]{3,2,1,0:T(8,128)S(1)}, f32[2,2,64,64]{3,2,1,0:T(8,128)}, u32[]{:S(2)}) copy-start(f32[2,2,64,64]{3,2,1,0:T(8,128)} %param.13) | copy-start | bytes 196612
  6.5 44.4 %copy-start.4 = (f32[2,2,64,64]{3,2,1,0:T(8,128)S(1)}, f32[2,2,64,64]{3,2,1,0:T(8,128)}, u32[]{:S(2)}) copy-start(f32[2,2,64,64]{3,2,1,0:T(8,128)} %param.15) | copy-start | bytes 196612
  6.5 44.9 %copy-start.6 = (f32[2,2,64]{2,1,0:T(2,128)S(1)}, f32[2,2,64]{2,1,0:T(2,128)}, u32[]{:S(2)}) copy-start(f32[2,2,64]{2,1,0:T(2,128)} %param.14) | copy-start | bytes 3076
  6.5 45.3 %copy-start.7 = (f32[2,2,64]{2,1,0:T(2,128)S(1)}, f32[2,2,64]{2,1,0:T(2,128)}, u32[]{:S(2)}) copy-start(f32[2,2,64]{2,1,0:T(2,128)} %param.16) | copy-start | bytes 3076
  38.3 41.4 %all-to-all-start = ((f32[2,8,256,128]{3,1,0,2:T(8,128)}), f32[2,8,256,128]{3,1,0,2:T(8,128)S(1)}, u32[]{:S(2)}, u32[]{:S(2)}) async-start(f32[2,8,256,128]{3,1,0,2:T(8,128)} %copy.50), calls=%async_computation | async-start | bytes 4194304 | tf_op jit(solution)/shard_map/all_to_all | solution.py:154
  141.0 37.3 %copy-start.11 = (f32[128]{0:T(128)S(1)}, f32[128]{0:T(128)}, u32[]{:S(2)}) copy-start(f32[128]{0:T(128)} %param.12) | copy-start | bytes 1540
  142.7 33.8 %all-to-all-start.1 = ((f32[2,512,4,128]{3,2,0,1:T(4,128)}), f32[2,512,4,128]{3,2,0,1:T(4,128)S(1)}, u32[]{:S(2)}, u32[]{:S(2)}) async-start(f32[2,512,4,128]{3,2,0,1:T(4,128)} %copy.78), calls=%async_computation.1 | async-start | bytes 4194304 | tf_op jit(solution)/shard_map/all_to_all | solution.py:161
  176.5 1.8 copy-start.2
  176.5 1.8 copy-start.3
  182.3 8.4 %copy-start.8 = (bf16[512]{0:T(512)(128)(2,1)S(1)}, bf16[512]{0:T(512)(128)(2,1)}, u32[]{:S(2)}) copy-start(bf16[512]{0:T(512)(128)(2,1)} %param.19) | copy-start | bytes 3076
  185.5 98.5 %all-to-all-start.2 = ((bf16[4,8,512,128]{2,1,3,0:T(8,128)(2,1)}), bf16[4,8,512,128]{2,1,3,0:T(8,128)(2,1)}, u32[]{:S(2)}, u32[]{:S(2)}) async-start(bf16[4,8,512,128]{2,1,3,0:T(8,128)(2,1)} %stack.11), calls=%async_computation.2 | async-start | bytes 8388608 | tf_op jit(solution)/shard_map/all_to_all | solution.py:13
  190.4 232.0 %reduce-scatter.4.cloned.1.call-start = ((), (), s32[]{:S(2)}) async-start(), calls=%async_computation.4 | async-start | bytes 5242880
  290.8 11.4 %copy-start.9 = (bf16[512,512]{1,0:T(8,128)(2,1)S(1)}, bf16[512,512]{1,0:T(8,128)(2,1)}, u32[]{:S(2)}) copy-start(bf16[512,512]{1,0:T(8,128)(2,1)} %param.18) | copy-start | bytes 1572868
  290.8 11.4 %copy-start.10 = (f32[512]{0:T(512)S(1)}, f32[512]{0:T(512)}, u32[]{:S(2)}) copy-start(f32[512]{0:T(512)} %param.17) | copy-start | bytes 6148
  335.7 6.5 %copy-start.12 = (bf16[128]{0:T(256)(128)(2,1)S(1)}, bf16[128]{0:T(256)(128)(2,1)}, u32[]{:S(2)}) copy-start(bf16[128]{0:T(256)(128)(2,1)} %param.21) | copy-start | bytes 772
  335.7 92.5 %copy-start.1 = (bf16[512,512]{1,0:T(8,128)(2,1)S(1)}, bf16[512,512]{1,0:T(8,128)(2,1)}, u32[]{:S(2)}) copy-start(bf16[512,512]{1,0:T(8,128)(2,1)} %param.20) | copy-start | bytes 1572868
Sparse Core Ops, SparseCore 0:
  342.4 79.9 reduce-scatter.3
